TPU v7x, 32 devices: a whole 2x2x4 slice. The times are simulated.
32 devices in a mesh: site: 4 (over y, x), bond: 8 (over z, core).
Axes of the slice: x: 2, y: 2, z: 4, core: 2. Of those that a mesh axis runs over, the one named last changes fastest.
Arguments:
- start_rows: bfloat16 [1024, 4096], P(None, 'bond'), may hold values from -6 to 6
- site_tensors: bfloat16 [4, 4096, 8, 4096], P('site', None, None, 'bond'), may hold values from -0.09375 to 0.09375
- block_scales: float32 [4, 8, 32], P('site', None, 'bond'), may hold values from 0.25 to 1
- displacement: float32 [4, 8, 8], P('site'), may hold values from -0.9 to 0.9
- outcomes: int32 [4, 1024], P('site'), may hold values from 0 to 7
Outputs:
- leaving: bfloat16 [4, 1024, 4096], P('site', None, 'bond')
- log_norms: float32 [4, 1024], P('site')
Inputs may be any that keep to these rules, and one draw needn't show every extreme that they name: outcomes index the second dimension of displacement.
All inputs are finite; a program needn't handle non-finite values.
Results may differ from a plain program's by a relative error of at most 0.014.
Values may be sent and summed in bfloat16 or wider, within the bound.
A program may use at most 128 MiB of HBM per device.

v0:
```python
import jax
import jax.numpy as jnp
from jax import lax
from jax.sharding import PartitionSpec as P

ROWS = 512


def shifted(value, axis, steps):
    count = lax.axis_size(axis)
    initial, last = (max(0, -steps), min(count, count - steps))
    return lax.ppermute(value, axis, [(source, source + steps) for source in range(initial, last)])


def local(start_rows, site_tensors, block_scales, displacement, outcomes):
    sites = lax.axis_size("site")
    cols = site_tensors.shape[3]
    chi = site_tensors.shape[1]
    phys = site_tensors.shape[2]
    nblk = block_scales.shape[2]
    allrows = start_rows.shape[0]
    grows = ROWS
    ngroups = allrows // grows
    ticks = ngroups + sites - 1
    a_mat = site_tensors[0].reshape(chi, phys * cols)
    scales = block_scales[0][:, :, None]
    table = displacement[0]
    outcome_row = outcomes[0]
    position = lax.axis_index("site")

    def tick(step, carry):
        incoming, incoming_norm, out_leave, out_logs = carry
        batch = step - position
        valid = jnp.logical_and(batch >= 0, batch < ngroups)
        first = jnp.clip(batch, 0, ngroups - 1) * grows
        start_piece = lax.dynamic_slice_in_dim(start_rows, first, grows, 0)
        rows_in = jnp.where(position == 0, start_piece, incoming)
        piece = lax.all_gather(rows_in, "bond", axis=1, tiled=True)
        total = jnp.dot(piece, a_mat, preferred_element_type=jnp.float32)
        pf = piece.astype(jnp.float32)
        total, squares = (total, jnp.sum(pf * pf, axis=1))
        local_norm = jnp.sqrt(squares / chi + 1e-06)
        prod = total.reshape(grows, phys, nblk, cols // nblk) * scales[None]
        prod = prod.reshape(grows, phys, cols)
        picked = lax.dynamic_slice_in_dim(outcome_row, first, grows, 0)
        onehot = (picked[:, None] == jnp.arange(phys, dtype=jnp.int32)[None, :]).astype(jnp.float32)
        weight = jnp.dot(onehot, table, precision=lax.Precision.HIGHEST)
        mixed = jnp.sum(weight[:, :, None] * prod, axis=1)
        leave = (mixed / local_norm[:, None]).astype(jnp.bfloat16)
        out_leave = jnp.where(
            valid, lax.dynamic_update_slice_in_dim(out_leave, leave, first, 0), out_leave
        )
        out_logs = jnp.where(
            valid,
            lax.dynamic_update_slice_in_dim(out_logs, jnp.log(local_norm), first, 0),
            out_logs,
        )
        incoming = shifted(leave, "site", 1)
        return (incoming, incoming_norm, out_leave, out_logs)

    carry = (
        jnp.zeros((grows, cols), jnp.bfloat16),
        jnp.ones((grows,), jnp.float32),
        jnp.zeros((allrows, cols), jnp.bfloat16),
        jnp.zeros((allrows,), jnp.float32),
    )
    carry = lax.fori_loop(0, ticks, tick, carry)
    return (carry[2][None], carry[3][None])


def solution(mesh):
    return jax.shard_map(
        local,
        mesh=mesh,
        in_specs=(
            P(None, "bond"),
            P("site", None, None, "bond"),
            P("site", None, "bond"),
            P("site", None, None),
            P("site", None),
        ),
        out_specs=(P("site", None, "bond"), P("site", None)),
        check_vma=False,
    )
```

profile of v0, /device:TPU:4, one launch (start us, length us, event | category | flops | bytes accessed | tf_op | source)
XLA Modules:
  0.0 550.5 jit_solution(6089565585654436752)
XLA Ops:
  7.2 22.7 %copy.10 = bf16[512,8,8,512]{3,1,2,0:T(8,128)(2,1)} copy(bf16[512,8,8,512]{3,2,1,0:T(8,128)(2,1)} %bitcast.35) | data formatting | bytes 67108864
  29.9 1.0 broadcast_in_dim.28
  31.1 512.3 %while.18 = (s32[]{:T(128)}, bf16[512,512]{1,0:T(8,128)(2,1)S(1)}, bf16[1024,512]{1,0:T(8,128)(2,1)}, f32[1024]{0:T(1024)S(1)}, s32[]{:T(128)}, /*index=5*/s32[1...) while((s32[]{:T(128)}, bf16[512,512]{1,0:T(8,128)(2,1)S(1)}, ...), condition=%wide.region_3.4_spmd, body=%wide.region_0.3_spmd.sunk | while | flops 17193637888 | bytes 113855224 | solution.py:67
  31.1 2.0 dynamic-slice_select_fusion.2
  33.2 0.1 dynamic_slice.20
  33.3 0.3 fusion.19
  33.6 47.9 %all-gather.2.cloned.1.call-done = bf16[512,4096]{1,0:T(8,128)(2,1)} async-done(((bf16[512,512]{1,0:T(8,128)(2,1)}), bf16[512,4096]{1,0:T(8,128)(2,1)}) %all-gather.2.cloned.1.call-update) | async-done | bytes 4194320 | tf_op jit(solution)/shard_map/while/body/eval_jaxpr/all_gather | solution.py:38
  81.6 22.6 %fusion.18 = f32[512,4096]{1,0:T(8,128)S(1)} fusion(bf16[512,4096]{1,0:T(8,128)(2,1)} %all-gather.2.cloned.1.call-done, bf16[4096,4096]{1,0:T(8,128)(2,1)} %get-tuple-element.361), kind=kOutput, calls=%fused_computation.14.clone.1 | convolution fusion | flops 17179869184 | bytes 46137344 | tf_op jit(solution)/shard_map/while/body/eval_jaxpr/dot_general | solution.py:39
  104.2 8.2 %copy.12 = f32[64,8,8,512]{3,2,1,0:T(8,128)S(1)} copy(f32[64,8,8,512]{3,1,2,0:T(8,128)S(1)} %bitcast.34) | data formatting | bytes 16777216 | tf_op jit(solution)/shard_map/while
  112.4 0.9 multiply_reduce_fusion.2
  113.3 0.2 select_dynamic-update-slice_fusion.4
  113.5 3.9 fusion.20
  117.4 2.1 select_dynamic-update-slice_fusion.5
  119.4 3.4 collective-permute-start
  122.8 13.5 %collective-permute-done = bf16[512,512]{1,0:T(8,128)(2,1)S(1)} collective-permute-done((bf16[512,512]{1,0:T(8,128)(2,1)S(1)}, bf16[512,512]{1,0:T(8,128)(2,1)S(1)}, u32[]{:S(2)}, u32[]{:S(2)}) %collective-permute-start) | collective-permute-done | bytes 524320 | tf_op jit(solution)/shard_map/while/body/eval_jaxpr/ppermute | solution.py:12
  136.3 2.0 dynamic-slice_select_fusion.2
  138.3 0.1 dynamic_slice.20
  138.5 0.3 fusion.19
  138.8 44.7 %all-gather.2.cloned.1.call-done = bf16[512,4096]{1,0:T(8,128)(2,1)} async-done(((bf16[512,512]{1,0:T(8,128)(2,1)}), bf16[512,4096]{1,0:T(8,128)(2,1)}) %all-gather.2.cloned.1.call-update) | async-done | bytes 4194320 | tf_op jit(solution)/shard_map/while/body/eval_jaxpr/all_gather | solution.py:38
  183.5 22.6 %fusion.18 = f32[512,4096]{1,0:T(8,128)S(1)} fusion(bf16[512,4096]{1,0:T(8,128)(2,1)} %all-gather.2.cloned.1.call-done, bf16[4096,4096]{1,0:T(8,128)(2,1)} %get-tuple-element.361), kind=kOutput, calls=%fused_computation.14.clone.1 | convolution fusion | flops 17179869184 | bytes 46137344 | tf_op jit(solution)/shard_map/while/body/eval_jaxpr/dot_general | solution.py:39
  206.1 8.2 %copy.12 = f32[64,8,8,512]{3,2,1,0:T(8,128)S(1)} copy(f32[64,8,8,512]{3,1,2,0:T(8,128)S(1)} %bitcast.34) | data formatting | bytes 16777216 | tf_op jit(solution)/shard_map/while
  214.3 0.9 multiply_reduce_fusion.2
  215.2 0.2 select_dynamic-update-slice_fusion.4
  215.4 3.9 fusion.20
  219.3 2.1 select_dynamic-update-slice_fusion.5
  221.4 3.4 collective-permute-start
  224.7 13.5 %collective-permute-done = bf16[512,512]{1,0:T(8,128)(2,1)S(1)} collective-permute-done((bf16[512,512]{1,0:T(8,128)(2,1)S(1)}, bf16[512,512]{1,0:T(8,128)(2,1)S(1)}, u32[]{:S(2)}, u32[]{:S(2)}) %collective-permute-start) | collective-permute-done | bytes 524320 | tf_op jit(solution)/shard_map/while/body/eval_jaxpr/ppermute | solution.py:12
  238.2 2.0 dynamic-slice_select_fusion.2
  240.2 0.1 dynamic_slice.20
  240.4 0.3 fusion.19
  240.7 44.7 %all-gather.2.cloned.1.call-done = bf16[512,4096]{1,0:T(8,128)(2,1)} async-done(((bf16[512,512]{1,0:T(8,128)(2,1)}), bf16[512,4096]{1,0:T(8,128)(2,1)}) %all-gather.2.cloned.1.call-update) | async-done | bytes 4194320 | tf_op jit(solution)/shard_map/while/body/eval_jaxpr/all_gather | solution.py:38
  285.4 22.6 %fusion.18 = f32[512,4096]{1,0:T(8,128)S(1)} fusion(bf16[512,4096]{1,0:T(8,128)(2,1)} %all-gather.2.cloned.1.call-done, bf16[4096,4096]{1,0:T(8,128)(2,1)} %get-tuple-element.361), kind=kOutput, calls=%fused_computation.14.clone.1 | convolution fusion | flops 17179869184 | bytes 46137344 | tf_op jit(solution)/shard_map/while/body/eval_jaxpr/dot_general | solution.py:39
  308.0 8.2 %copy.12 = f32[64,8,8,512]{3,2,1,0:T(8,128)S(1)} copy(f32[64,8,8,512]{3,1,2,0:T(8,128)S(1)} %bitcast.34) | data formatting | bytes 16777216 | tf_op jit(solution)/shard_map/while
  316.2 0.9 multiply_reduce_fusion.2
  317.1 0.2 select_dynamic-update-slice_fusion.4
  317.3 3.9 fusion.20
  321.2 2.1 select_dynamic-update-slice_fusion.5
  323.3 3.4 collective-permute-start
  326.6 13.5 %collective-permute-done = bf16[512,512]{1,0:T(8,128)(2,1)S(1)} collective-permute-done((bf16[512,512]{1,0:T(8,128)(2,1)S(1)}, bf16[512,512]{1,0:T(8,128)(2,1)S(1)}, u32[]{:S(2)}, u32[]{:S(2)}) %collective-permute-start) | collective-permute-done | bytes 524320 | tf_op jit(solution)/shard_map/while/body/eval_jaxpr/ppermute | solution.py:12
  340.1 2.0 dynamic-slice_select_fusion.2
  342.1 0.1 dynamic_slice.20
  342.3 0.3 fusion.19
  342.6 44.4 %all-gather.2.cloned.1.call-done = bf16[512,4096]{1,0:T(8,128)(2,1)} async-done(((bf16[512,512]{1,0:T(8,128)(2,1)}), bf16[512,4096]{1,0:T(8,128)(2,1)}) %all-gather.2.cloned.1.call-update) | async-done | bytes 4194320 | tf_op jit(solution)/shard_map/while/body/eval_jaxpr/all_gather | solution.py:38
  387.0 22.6 %fusion.18 = f32[512,4096]{1,0:T(8,128)S(1)} fusion(bf16[512,4096]{1,0:T(8,128)(2,1)} %all-gather.2.cloned.1.call-done, bf16[4096,4096]{1,0:T(8,128)(2,1)} %get-tuple-element.361), kind=kOutput, calls=%fused_computation.14.clone.1 | convolution fusion | flops 17179869184 | bytes 46137344 | tf_op jit(solution)/shard_map/while/body/eval_jaxpr/dot_general | solution.py:39
  409.7 8.2 %copy.12 = f32[64,8,8,512]{3,2,1,0:T(8,128)S(1)} copy(f32[64,8,8,512]{3,1,2,0:T(8,128)S(1)} %bitcast.34) | data formatting | bytes 16777216 | tf_op jit(solution)/shard_map/while
  417.8 0.9 multiply_reduce_fusion.2
  418.7 0.2 select_dynamic-update-slice_fusion.4
  418.9 3.9 fusion.20
  422.8 2.1 select_dynamic-update-slice_fusion.5
  424.9 3.4 collective-permute-start
  428.3 13.5 %collective-permute-done = bf16[512,512]{1,0:T(8,128)(2,1)S(1)} collective-permute-done((bf16[512,512]{1,0:T(8,128)(2,1)S(1)}, bf16[512,512]{1,0:T(8,128)(2,1)S(1)}, u32[]{:S(2)}, u32[]{:S(2)}) %collective-permute-start) | collective-permute-done | bytes 524320 | tf_op jit(solution)/shard_map/while/body/eval_jaxpr/ppermute | solution.py:12
  441.7 2.0 dynamic-slice_select_fusion.2
  443.8 0.1 dynamic_slice.20
  443.9 0.3 fusion.19
  444.2 44.4 %all-gather.2.cloned.1.call-done = bf16[512,4096]{1,0:T(8,128)(2,1)} async-done(((bf16[512,512]{1,0:T(8,128)(2,1)}), bf16[512,4096]{1,0:T(8,128)(2,1)}) %all-gather.2.cloned.1.call-update) | async-done | bytes 4194320 | tf_op jit(solution)/shard_map/while/body/eval_jaxpr/all_gather | solution.py:38
  488.7 22.6 %fusion.18 = f32[512,4096]{1,0:T(8,128)S(1)} fusion(bf16[512,4096]{1,0:T(8,128)(2,1)} %all-gather.2.cloned.1.call-done, bf16[4096,4096]{1,0:T(8,128)(2,1)} %get-tuple-element.361), kind=kOutput, calls=%fused_computation.14.clone.1 | convolution fusion | flops 17179869184 | bytes 46137344 | tf_op jit(solution)/shard_map/while/body/eval_jaxpr/dot_general | solution.py:39
  511.3 8.2 %copy.12 = f32[64,8,8,512]{3,2,1,0:T(8,128)S(1)} copy(f32[64,8,8,512]{3,1,2,0:T(8,128)S(1)} %bitcast.34) | data formatting | bytes 16777216 | tf_op jit(solution)/shard_map/while
  519.5 0.9 multiply_reduce_fusion.2
  520.4 0.2 select_dynamic-update-slice_fusion.4
  520.6 3.9 fusion.20
  524.5 2.1 select_dynamic-update-slice_fusion.5
  526.5 3.4 collective-permute-start
  529.9 13.5 %collective-permute-done = bf16[512,512]{1,0:T(8,128)(2,1)S(1)} collective-permute-done((bf16[512,512]{1,0:T(8,128)(2,1)S(1)}, bf16[512,512]{1,0:T(8,128)(2,1)S(1)}, u32[]{:S(2)}, u32[]{:S(2)}) %collective-permute-start) | collective-permute-done | bytes 524320 | tf_op jit(solution)/shard_map/while/body/eval_jaxpr/ppermute | solution.py:12
  543.4 0.6 copy-done.3
  (34 shorter events, 0.6 us)
Async XLA Ops:
  7.2 23.9 %copy-start.1 = (f32[1,8,8]{2,1,0:T(8,128)S(1)}, f32[1,8,8]{2,1,0:T(8,128)}, u32[]{:S(2)}) copy-start(f32[1,8,8]{2,1,0:T(8,128)} %param.10) | copy-start | bytes 772
  7.2 23.9 %copy-start.2 = (f32[1,8,4]{1,2,0:T(4,128)S(1)}, f32[1,8,4]{1,2,0:T(4,128)}, u32[]{:S(2)}) copy-start(f32[1,8,4]{1,2,0:T(4,128)} %param.9) | copy-start | bytes 388
  7.2 23.9 %copy-start.4 = (s32[1,1024]{1,0:T(1,128)S(1)}, s32[1,1024]{1,0:T(1,128)}, u32[]{:S(2)}) copy-start(s32[1,1024]{1,0:T(1,128)} %param.11) | copy-start | bytes 12292
  31.1 50.5 %all-gather.2.cloned.1.call-start = ((), (), s32[]{:S(2)}) async-start(), calls=%async_computation | async-start | bytes 4718592 | tf_op jit(solution)/shard_map/while/body/eval_jaxpr/all_gather | solution.py:38
  104.2 8.2 %copy-start = (bf16[512,4096]{1,0:T(8,128)(2,1)S(1)}, bf16[512,4096]{1,0:T(8,128)(2,1)}, u32[]{:S(2)}) copy-start(bf16[512,4096]{1,0:T(8,128)(2,1)} %all-gather.2.cloned.1.call-done) | copy-start | bytes 12582916 | tf_op jit(solution)/shard_map/while
  119.4 16.8 %collective-permute-start = (bf16[512,512]{1,0:T(8,128)(2,1)S(1)}, bf16[512,512]{1,0:T(8,128)(2,1)S(1)}, u32[]{:S(2)}, u32[]{:S(2)}) collective-permute-start(bf16[512,512]{1,0:T(8,128)(2,1)S(1)} %get-tuple-element.317), channel_id=1, source_target_pairs={{0,8},{8,16},{16,24},{1,9},{9,17},{17,25},{2,10},{10,18},{18,26},{... | collective-permute-start | bytes 1572872 | tf_op jit(solution)/shard_map/while/body/eval_jaxpr/ppermute | solution.py:12
  136.3 47.2 %all-gather.2.cloned.1.call-start = ((), (), s32[]{:S(2)}) async-start(), calls=%async_computation | async-start | bytes 4718592 | tf_op jit(solution)/shard_map/while/body/eval_jaxpr/all_gather | solution.py:38
  206.1 8.2 %copy-start = (bf16[512,4096]{1,0:T(8,128)(2,1)S(1)}, bf16[512,4096]{1,0:T(8,128)(2,1)}, u32[]{:S(2)}) copy-start(bf16[512,4096]{1,0:T(8,128)(2,1)} %all-gather.2.cloned.1.call-done) | copy-start | bytes 12582916 | tf_op jit(solution)/shard_map/while
  221.4 16.8 %collective-permute-start = (bf16[512,512]{1,0:T(8,128)(2,1)S(1)}, bf16[512,512]{1,0:T(8,128)(2,1)S(1)}, u32[]{:S(2)}, u32[]{:S(2)}) collective-permute-start(bf16[512,512]{1,0:T(8,128)(2,1)S(1)} %get-tuple-element.317), channel_id=1, source_target_pairs={{0,8},{8,16},{16,24},{1,9},{9,17},{17,25},{2,10},{10,18},{18,26},{... | collective-permute-start | bytes 1572872 | tf_op jit(solution)/shard_map/while/body/eval_jaxpr/ppermute | solution.py:12
  238.2 47.2 %all-gather.2.cloned.1.call-start = ((), (), s32[]{:S(2)}) async-start(), calls=%async_computation | async-start | bytes 4718592 | tf_op jit(solution)/shard_map/while/body/eval_jaxpr/all_gather | solution.py:38
  308.0 8.2 %copy-start = (bf16[512,4096]{1,0:T(8,128)(2,1)S(1)}, bf16[512,4096]{1,0:T(8,128)(2,1)}, u32[]{:S(2)}) copy-start(bf16[512,4096]{1,0:T(8,128)(2,1)} %all-gather.2.cloned.1.call-done) | copy-start | bytes 12582916 | tf_op jit(solution)/shard_map/while
  323.3 16.8 %collective-permute-start = (bf16[512,512]{1,0:T(8,128)(2,1)S(1)}, bf16[512,512]{1,0:T(8,128)(2,1)S(1)}, u32[]{:S(2)}, u32[]{:S(2)}) collective-permute-start(bf16[512,512]{1,0:T(8,128)(2,1)S(1)} %get-tuple-element.317), channel_id=1, source_target_pairs={{0,8},{8,16},{16,24},{1,9},{9,17},{17,25},{2,10},{10,18},{18,26},{... | collective-permute-start | bytes 1572872 | tf_op jit(solution)/shard_map/while/body/eval_jaxpr/ppermute | solution.py:12
  340.1 46.9 %all-gather.2.cloned.1.call-start = ((), (), s32[]{:S(2)}) async-start(), calls=%async_computation | async-start | bytes 4718592 | tf_op jit(solution)/shard_map/while/body/eval_jaxpr/all_gather | solution.py:38
  409.6 8.2 %copy-start = (bf16[512,4096]{1,0:T(8,128)(2,1)S(1)}, bf16[512,4096]{1,0:T(8,128)(2,1)}, u32[]{:S(2)}) copy-start(bf16[512,4096]{1,0:T(8,128)(2,1)} %all-gather.2.cloned.1.call-done) | copy-start | bytes 12582916 | tf_op jit(solution)/shard_map/while
  424.9 16.8 %collective-permute-start = (bf16[512,512]{1,0:T(8,128)(2,1)S(1)}, bf16[512,512]{1,0:T(8,128)(2,1)S(1)}, u32[]{:S(2)}, u32[]{:S(2)}) collective-permute-start(bf16[512,512]{1,0:T(8,128)(2,1)S(1)} %get-tuple-element.317), channel_id=1, source_target_pairs={{0,8},{8,16},{16,24},{1,9},{9,17},{17,25},{2,10},{10,18},{18,26},{... | collective-permute-start | bytes 1572872 | tf_op jit(solution)/shard_map/while/body/eval_jaxpr/ppermute | solution.py:12
  441.7 46.9 %all-gather.2.cloned.1.call-start = ((), (), s32[]{:S(2)}) async-start(), calls=%async_computation | async-start | bytes 4718592 | tf_op jit(solution)/shard_map/while/body/eval_jaxpr/all_gather | solution.py:38
  511.3 8.2 %copy-start = (bf16[512,4096]{1,0:T(8,128)(2,1)S(1)}, bf16[512,4096]{1,0:T(8,128)(2,1)}, u32[]{:S(2)}) copy-start(bf16[512,4096]{1,0:T(8,128)(2,1)} %all-gather.2.cloned.1.call-done) | copy-start | bytes 12582916 | tf_op jit(solution)/shard_map/while
  526.5 16.8 %collective-permute-start = (bf16[512,512]{1,0:T(8,128)(2,1)S(1)}, bf16[512,512]{1,0:T(8,128)(2,1)S(1)}, u32[]{:S(2)}, u32[]{:S(2)}) collective-permute-start(bf16[512,512]{1,0:T(8,128)(2,1)S(1)} %get-tuple-element.317), channel_id=1, source_target_pairs={{0,8},{8,16},{16,24},{1,9},{9,17},{17,25},{2,10},{10,18},{18,26},{... | collective-permute-start | bytes 1572872 | tf_op jit(solution)/shard_map/while/body/eval_jaxpr/ppermute | solution.py:12
  543.4 0.6 copy-start.3
Sparse Core Ops, SparseCore 0:
  33.5 48.0 all-gather.1
  138.7 44.7 all-gather.1
  240.6 44.7 all-gather.1
  342.2 44.7 all-gather.1
  443.9 44.7 all-gather.1
where the time goes:
time: 551 us
  waiting for transfers between devices  294 us (53%)
  matrix products  115 us (21%)
  local copies, waits for them, and re-layouts  66 us (12%)
  other arithmetic  45.2 us (8%)
  starting transfers between devices  16.9 us (3%)
  between operations  13.8 us (3%)
    all_gather x5, waiting for transfers between devices, tick(): piece = lax.all_gather(rows_in, 'bond', axis=1, tiled=True)  226 us
    dot_general x5, matrix products, tick(): total = jnp.dot(piece, a_mat, preferred_element_type=jnp.float32)  113 us
    ppermute x5, waiting for transfers between devices, shifted(): lax.ppermute(value, axis, [(source, source + steps) for source in range(i...  67.3 us
    while x15, local copies, waits for them, and re-layouts  40.9 us
    unnamed x9, local copies, waits for them, and re-layouts  23.3 us
    reduce_sum x5, other arithmetic, tick(): mixed = jnp.sum(weight[:, :, None] * prod, axis=1)  19.5 us
    ppermute x5, starting transfers between devices, shifted(): lax.ppermute(value, axis, [(source, source + steps) for source in range(i...  16.8 us
  transfers between devices with their start and end apart: 10, of which 10 were waited for; matrix products, arithmetic and copies ran while one was open for 0% of the time, Pallas kernels for 0%

commit v1 on v0

--- a/solution.py
+++ b/solution.py
@@ -4,6 +4,19 @@
 from jax.sharding import PartitionSpec as P
 
 ROWS = 512
+
+
+def ring_gather(value, axis, dim):
+    ways = lax.axis_size(axis)
+    up = [(d, (d + 1) % ways) for d in range(ways)]
+    down = [(d, (d - 1) % ways) for d in range(ways)]
+    earlier, later = ([value], [value])
+    for _ in range(ways // 2):
+        earlier.append(lax.ppermute(earlier[-1], axis, up))
+    for _ in range((ways - 1) // 2):
+        later.append(lax.ppermute(later[-1], axis, down))
+    line = jnp.concatenate([*earlier[::-1], *later[1:]], axis=dim)
+    return jnp.roll(line, (lax.axis_index(axis) - ways // 2) * value.shape[dim], axis=dim)
 
 
 def shifted(value, axis, steps):
@@ -35,7 +48,7 @@
         first = jnp.clip(batch, 0, ngroups - 1) * grows
         start_piece = lax.dynamic_slice_in_dim(start_rows, first, grows, 0)
         rows_in = jnp.where(position == 0, start_piece, incoming)
-        piece = lax.all_gather(rows_in, "bond", axis=1, tiled=True)
+        piece = ring_gather(rows_in, "bond", 1)
         total = jnp.dot(piece, a_mat, preferred_element_type=jnp.float32)
         pf = piece.astype(jnp.float32)
         total, squares = (total, jnp.sum(pf * pf, axis=1))

time: 551 us -> 531 us (0.964)
  waiting for transfers between devices: 294 us -> 239 us
  starting transfers between devices: 16.9 us -> 67.2 us
  local copies, waits for them, and re-layouts: 66 us -> 80.8 us
  other arithmetic: 45.2 us -> 32 us
  between operations: 13.8 us -> 0.67 us
    all_gather x5 -> x0, waiting for transfers between devices: 226 us -> none  [tick(): piece = lax.all_gather(rows_in, 'bond', axis=1, tiled=True)]
    ppermute x0 -> x35, waiting for transfers between devices: none -> 190 us  [the longest x20 179 us: ring_gather(): earlier.append(lax.ppermute(earlier[-1], axis, up))]
    ppermute x0 -> x35, starting transfers between devices: none -> 55.5 us  [the longest x15 55.2 us: ring_gather(): later.append(lax.ppermute(later[-1], axis, down))]
    ppermute x5, waiting for transfers between devices: 67.3 us -> 48.2 us  [shifted(): lax.ppermute(value, axis, [(source, source + steps) for source in range(i...]
    while x15 -> x100, local copies, waits for them, and re-layouts: 40.9 us -> 55.4 us
    select_n x5, other arithmetic: 10.4 us -> 1.24 us  [tick(): jnp.where(valid, lax.dynamic_update_slice_in_dim(out_leave, leave, first,...]
  transfers between devices with their start and end apart: 10 -> 40, of which waited for: 10 -> 34; matrix products, arithmetic and copies ran while one was open for 0% -> 2% of each run, Pallas kernels for 0% -> 0%
where the time goes in v1:
time: 531 us; the launch traced here: 530 us
  waiting for transfers between devices  239 us (45%)
  matrix products  110 us (21%)
  local copies, waits for them, and re-layouts  80.8 us (15%)
  starting transfers between devices  67.2 us (13%)
  other arithmetic  32 us (6%)
    ppermute x20, waiting for transfers between devices, ring_gather(): earlier.append(lax.ppermute(earlier[-1], axis, up))  179 us
    dot_general x5, matrix products, tick(): total = jnp.dot(piece, a_mat, preferred_element_type=jnp.float32)  108 us
    while x100, local copies, waits for them, and re-layouts  55.4 us
    ppermute x15, starting transfers between devices, ring_gather(): later.append(lax.ppermute(later[-1], axis, down))  55.2 us
    ppermute x5, waiting for transfers between devices, shifted(): lax.ppermute(value, axis, [(source, source + steps) for source in range(i...  48.2 us
    unnamed x9, local copies, waits for them, and re-layouts  23.3 us
    reduce_sum x5, other arithmetic, tick(): mixed = jnp.sum(weight[:, :, None] * prod, axis=1)  19.5 us
    ppermute x5, starting transfers between devices, shifted(): lax.ppermute(value, axis, [(source, source + steps) for source in range(i...  11.7 us
  transfers between devices with their start and end apart: 40, of which 34 were waited for; matrix products, arithmetic and copies ran while one was open for 2% of the time, Pallas kernels for 0%

profile of v1, /device:TPU:4, one launch (start us, length us, event | category | flops | bytes accessed | tf_op | source)
XLA Modules:
  0.0 530.2 jit_solution(11247330403048292650)
XLA Ops:
  0.7 22.7 %copy.10 = bf16[512,8,8,512]{3,1,2,0:T(8,128)(2,1)} copy(bf16[512,8,8,512]{3,2,1,0:T(8,128)(2,1)} %bitcast.32) | data formatting | bytes 67108864
  24.5 505.1 %while.19 = (s32[]{:T(128)}, bf16[512,512]{1,0:T(8,128)(2,1)S(1)}, bf16[1024,512]{1,0:T(8,128)(2,1)}, f32[1024]{0:T(1024)S(1)}, s32[]{:T(128)}, /*index=5*/s32[1...) while((s32[]{:T(128)}, bf16[512,512]{1,0:T(8,128)(2,1)S(1)}, ...), condition=%wide.region_3.4_spmd, body=%wide.region_0.3_spmd.sunk | while | flops 17193637888 | bytes 122768632 | solution.py:80
  25.8 10.4 %collective-permute-done = bf16[512,512]{1,0:T(8,128)(2,1)S(1)} collective-permute-done((bf16[512,512]{1,0:T(8,128)(2,1)S(1)}, bf16[512,512]{1,0:T(8,128)(2,1)S(1)}, u32[]{:S(2)}, u32[]{:S(2)}) %collective-permute-start) | collective-permute-done | bytes 524320 | tf_op jit(solution)/shard_map/while/body/eval_jaxpr/ppermute | solution.py:15
  36.2 3.5 collective-permute-start.4
  39.7 12.2 %collective-permute-done.1 = bf16[512,512]{1,0:T(8,128)(2,1)S(1)} collective-permute-done((bf16[512,512]{1,0:T(8,128)(2,1)S(1)}, bf16[512,512]{1,0:T(8,128)(2,1)S(1)}, u32[]{:S(2)}, u32[]{:S(2)}) %collective-permute-start.1) | collective-permute-done | bytes 524320 | tf_op jit(solution)/shard_map/while/body/eval_jaxpr/ppermute | solution.py:15
  51.9 3.5 collective-permute-start.5
  55.4 11.1 %collective-permute-done.2 = bf16[512,512]{1,0:T(8,128)(2,1)S(1)} collective-permute-done((bf16[512,512]{1,0:T(8,128)(2,1)S(1)}, bf16[512,512]{1,0:T(8,128)(2,1)S(1)}, u32[]{:S(2)}, u32[]{:S(2)}) %collective-permute-start.2) | collective-permute-done | bytes 524320 | tf_op jit(solution)/shard_map/while/body/eval_jaxpr/ppermute | solution.py:15
  67.6 3.8 collective-permute-start.6
  71.4 8.3 %collective-permute-done.3 = bf16[512,512]{1,0:T(8,128)(2,1)} collective-permute-done((bf16[512,512]{1,0:T(8,128)(2,1)S(1)}, bf16[512,512]{1,0:T(8,128)(2,1)}, u32[]{:S(2)}, u32[]{:S(2)}) %collective-permute-start.3) | collective-permute-done | bytes 524320 | tf_op jit(solution)/shard_map/while/body/eval_jaxpr/ppermute | solution.py:15
  83.7 21.6 %fusion.19 = f32[512,4096]{1,0:T(8,128)S(1)} fusion(bf16[4096,4096]{1,0:T(8,128)(2,1)} %get-tuple-element.408, bf16[512,8192]{1,0:T(8,128)(2,1)S(1)} %constant_dynamic-update-slice_fusion.47, s32[]{:T(128)S(6)} %select_n.135), kind=kOutput, calls=%fused_computation.4.clone.1 | convolution fusion | flops 17179869184 | bytes 46137348 | tf_op jit(solution)/shard_map/while/body/eval_jaxpr/dot_general | solution.py:52
  105.3 8.1 %copy.12 = f32[64,8,8,512]{3,2,1,0:T(8,128)S(1)} copy(f32[64,8,8,512]{3,1,2,0:T(8,128)S(1)} %bitcast.31) | data formatting | bytes 16777216 | tf_op jit(solution)/shard_map/while
  113.5 3.9 fusion.21
  117.8 3.4 collective-permute-start.7
  121.2 8.6 %collective-permute-done.7 = bf16[512,512]{1,0:T(8,128)(2,1)S(1)} collective-permute-done((bf16[512,512]{1,0:T(8,128)(2,1)S(1)}, bf16[512,512]{1,0:T(8,128)(2,1)S(1)}, u32[]{:S(2)}, u32[]{:S(2)}) %collective-permute-start.7) | collective-permute-done | bytes 524320 | tf_op jit(solution)/shard_map/while/body/eval_jaxpr/ppermute | solution.py:25
  131.0 10.5 %collective-permute-done = bf16[512,512]{1,0:T(8,128)(2,1)S(1)} collective-permute-done((bf16[512,512]{1,0:T(8,128)(2,1)S(1)}, bf16[512,512]{1,0:T(8,128)(2,1)S(1)}, u32[]{:S(2)}, u32[]{:S(2)}) %collective-permute-start) | collective-permute-done | bytes 524320 | tf_op jit(solution)/shard_map/while/body/eval_jaxpr/ppermute | solution.py:15
  141.5 3.5 collective-permute-start.4
  145.1 8.9 %collective-permute-done.1 = bf16[512,512]{1,0:T(8,128)(2,1)S(1)} collective-permute-done((bf16[512,512]{1,0:T(8,128)(2,1)S(1)}, bf16[512,512]{1,0:T(8,128)(2,1)S(1)}, u32[]{:S(2)}, u32[]{:S(2)}) %collective-permute-start.1) | collective-permute-done | bytes 524320 | tf_op jit(solution)/shard_map/while/body/eval_jaxpr/ppermute | solution.py:15
  155.1 3.7 collective-permute-start.5
  158.8 7.7 %collective-permute-done.2 = bf16[512,512]{1,0:T(8,128)(2,1)S(1)} collective-permute-done((bf16[512,512]{1,0:T(8,128)(2,1)S(1)}, bf16[512,512]{1,0:T(8,128)(2,1)S(1)}, u32[]{:S(2)}, u32[]{:S(2)}) %collective-permute-start.2) | collective-permute-done | bytes 524320 | tf_op jit(solution)/shard_map/while/body/eval_jaxpr/ppermute | solution.py:15
  167.6 3.8 collective-permute-start.6
  171.4 8.2 %collective-permute-done.3 = bf16[512,512]{1,0:T(8,128)(2,1)} collective-permute-done((bf16[512,512]{1,0:T(8,128)(2,1)S(1)}, bf16[512,512]{1,0:T(8,128)(2,1)}, u32[]{:S(2)}, u32[]{:S(2)}) %collective-permute-start.3) | collective-permute-done | bytes 524320 | tf_op jit(solution)/shard_map/while/body/eval_jaxpr/ppermute | solution.py:15
  183.6 21.6 %fusion.19 = f32[512,4096]{1,0:T(8,128)S(1)} fusion(bf16[4096,4096]{1,0:T(8,128)(2,1)} %get-tuple-element.408, bf16[512,8192]{1,0:T(8,128)(2,1)S(1)} %constant_dynamic-update-slice_fusion.47, s32[]{:T(128)S(6)} %select_n.135), kind=kOutput, calls=%fused_computation.4.clone.1 | convolution fusion | flops 17179869184 | bytes 46137348 | tf_op jit(solution)/shard_map/while/body/eval_jaxpr/dot_general | solution.py:52
  205.2 8.1 %copy.12 = f32[64,8,8,512]{3,2,1,0:T(8,128)S(1)} copy(f32[64,8,8,512]{3,1,2,0:T(8,128)S(1)} %bitcast.31) | data formatting | bytes 16777216 | tf_op jit(solution)/shard_map/while
  213.3 3.9 fusion.21
  217.7 2.5 collective-permute-start.7
  220.2 9.5 %collective-permute-done.7 = bf16[512,512]{1,0:T(8,128)(2,1)S(1)} collective-permute-done((bf16[512,512]{1,0:T(8,128)(2,1)S(1)}, bf16[512,512]{1,0:T(8,128)(2,1)S(1)}, u32[]{:S(2)}, u32[]{:S(2)}) %collective-permute-start.7) | collective-permute-done | bytes 524320 | tf_op jit(solution)/shard_map/while/body/eval_jaxpr/ppermute | solution.py:25
  230.9 10.5 %collective-permute-done = bf16[512,512]{1,0:T(8,128)(2,1)S(1)} collective-permute-done((bf16[512,512]{1,0:T(8,128)(2,1)S(1)}, bf16[512,512]{1,0:T(8,128)(2,1)S(1)}, u32[]{:S(2)}, u32[]{:S(2)}) %collective-permute-start) | collective-permute-done | bytes 524320 | tf_op jit(solution)/shard_map/while/body/eval_jaxpr/ppermute | solution.py:15
  241.5 3.5 collective-permute-start.4
  245.0 8.9 %collective-permute-done.1 = bf16[512,512]{1,0:T(8,128)(2,1)S(1)} collective-permute-done((bf16[512,512]{1,0:T(8,128)(2,1)S(1)}, bf16[512,512]{1,0:T(8,128)(2,1)S(1)}, u32[]{:S(2)}, u32[]{:S(2)}) %collective-permute-start.1) | collective-permute-done | bytes 524320 | tf_op jit(solution)/shard_map/while/body/eval_jaxpr/ppermute | solution.py:15
  253.9 2.7 collective-permute-done.4
  256.6 3.8 collective-permute-start.5
  260.3 6.1 %collective-permute-done.2 = bf16[512,512]{1,0:T(8,128)(2,1)S(1)} collective-permute-done((bf16[512,512]{1,0:T(8,128)(2,1)S(1)}, bf16[512,512]{1,0:T(8,128)(2,1)S(1)}, u32[]{:S(2)}, u32[]{:S(2)}) %collective-permute-start.2) | collective-permute-done | bytes 524320 | tf_op jit(solution)/shard_map/while/body/eval_jaxpr/ppermute | solution.py:15
  266.9 3.1 collective-permute-done.5
  270.0 3.7 collective-permute-start.6
  273.7 5.7 %collective-permute-done.3 = bf16[512,512]{1,0:T(8,128)(2,1)} collective-permute-done((bf16[512,512]{1,0:T(8,128)(2,1)S(1)}, bf16[512,512]{1,0:T(8,128)(2,1)}, u32[]{:S(2)}, u32[]{:S(2)}) %collective-permute-start.3) | collective-permute-done | bytes 524320 | tf_op jit(solution)/shard_map/while/body/eval_jaxpr/ppermute | solution.py:15
  283.5 21.6 %fusion.19 = f32[512,4096]{1,0:T(8,128)S(1)} fusion(bf16[4096,4096]{1,0:T(8,128)(2,1)} %get-tuple-element.408, bf16[512,8192]{1,0:T(8,128)(2,1)S(1)} %constant_dynamic-update-slice_fusion.47, s32[]{:T(128)S(6)} %select_n.135), kind=kOutput, calls=%fused_computation.4.clone.1 | convolution fusion | flops 17179869184 | bytes 46137348 | tf_op jit(solution)/shard_map/while/body/eval_jaxpr/dot_general | solution.py:52
  305.1 8.1 %copy.12 = f32[64,8,8,512]{3,2,1,0:T(8,128)S(1)} copy(f32[64,8,8,512]{3,1,2,0:T(8,128)S(1)} %bitcast.31) | data formatting | bytes 16777216 | tf_op jit(solution)/shard_map/while
  313.2 3.9 fusion.21
  317.6 1.9 collective-permute-start.7
  319.5 10.0 %collective-permute-done.7 = bf16[512,512]{1,0:T(8,128)(2,1)S(1)} collective-permute-done((bf16[512,512]{1,0:T(8,128)(2,1)S(1)}, bf16[512,512]{1,0:T(8,128)(2,1)S(1)}, u32[]{:S(2)}, u32[]{:S(2)}) %collective-permute-start.7) | collective-permute-done | bytes 524320 | tf_op jit(solution)/shard_map/while/body/eval_jaxpr/ppermute | solution.py:25
  330.8 10.5 %collective-permute-done = bf16[512,512]{1,0:T(8,128)(2,1)S(1)} collective-permute-done((bf16[512,512]{1,0:T(8,128)(2,1)S(1)}, bf16[512,512]{1,0:T(8,128)(2,1)S(1)}, u32[]{:S(2)}, u32[]{:S(2)}) %collective-permute-start) | collective-permute-done | bytes 524320 | tf_op jit(solution)/shard_map/while/body/eval_jaxpr/ppermute | solution.py:15
  341.3 3.5 collective-permute-start.4
  344.9 9.0 %collective-permute-done.1 = bf16[512,512]{1,0:T(8,128)(2,1)S(1)} collective-permute-done((bf16[512,512]{1,0:T(8,128)(2,1)S(1)}, bf16[512,512]{1,0:T(8,128)(2,1)S(1)}, u32[]{:S(2)}, u32[]{:S(2)}) %collective-permute-start.1) | collective-permute-done | bytes 524320 | tf_op jit(solution)/shard_map/while/body/eval_jaxpr/ppermute | solution.py:15
  354.9 3.9 collective-permute-start.5
  358.8 7.6 %collective-permute-done.2 = bf16[512,512]{1,0:T(8,128)(2,1)S(1)} collective-permute-done((bf16[512,512]{1,0:T(8,128)(2,1)S(1)}, bf16[512,512]{1,0:T(8,128)(2,1)S(1)}, u32[]{:S(2)}, u32[]{:S(2)}) %collective-permute-start.2) | collective-permute-done | bytes 524320 | tf_op jit(solution)/shard_map/while/body/eval_jaxpr/ppermute | solution.py:15
  367.4 3.8 collective-permute-start.6
  371.2 8.2 %collective-permute-done.3 = bf16[512,512]{1,0:T(8,128)(2,1)} collective-permute-done((bf16[512,512]{1,0:T(8,128)(2,1)S(1)}, bf16[512,512]{1,0:T(8,128)(2,1)}, u32[]{:S(2)}, u32[]{:S(2)}) %collective-permute-start.3) | collective-permute-done | bytes 524320 | tf_op jit(solution)/shard_map/while/body/eval_jaxpr/ppermute | solution.py:15
  383.5 21.6 %fusion.19 = f32[512,4096]{1,0:T(8,128)S(1)} fusion(bf16[4096,4096]{1,0:T(8,128)(2,1)} %get-tuple-element.408, bf16[512,8192]{1,0:T(8,128)(2,1)S(1)} %constant_dynamic-update-slice_fusion.47, s32[]{:T(128)S(6)} %select_n.135), kind=kOutput, calls=%fused_computation.4.clone.1 | convolution fusion | flops 17179869184 | bytes 46137348 | tf_op jit(solution)/shard_map/while/body/eval_jaxpr/dot_general | solution.py:52
  405.1 8.1 %copy.12 = f32[64,8,8,512]{3,2,1,0:T(8,128)S(1)} copy(f32[64,8,8,512]{3,1,2,0:T(8,128)S(1)} %bitcast.31) | data formatting | bytes 16777216 | tf_op jit(solution)/shard_map/while
  413.2 3.9 fusion.21
  417.6 1.9 collective-permute-start.7
  419.5 10.0 %collective-permute-done.7 = bf16[512,512]{1,0:T(8,128)(2,1)S(1)} collective-permute-done((bf16[512,512]{1,0:T(8,128)(2,1)S(1)}, bf16[512,512]{1,0:T(8,128)(2,1)S(1)}, u32[]{:S(2)}, u32[]{:S(2)}) %collective-permute-start.7) | collective-permute-done | bytes 524320 | tf_op jit(solution)/shard_map/while/body/eval_jaxpr/ppermute | solution.py:25
  430.8 10.5 %collective-permute-done = bf16[512,512]{1,0:T(8,128)(2,1)S(1)} collective-permute-done((bf16[512,512]{1,0:T(8,128)(2,1)S(1)}, bf16[512,512]{1,0:T(8,128)(2,1)S(1)}, u32[]{:S(2)}, u32[]{:S(2)}) %collective-permute-start) | collective-permute-done | bytes 524320 | tf_op jit(solution)/shard_map/while/body/eval_jaxpr/ppermute | solution.py:15
  441.3 3.5 collective-permute-start.4
  444.8 9.0 %collective-permute-done.1 = bf16[512,512]{1,0:T(8,128)(2,1)S(1)} collective-permute-done((bf16[512,512]{1,0:T(8,128)(2,1)S(1)}, bf16[512,512]{1,0:T(8,128)(2,1)S(1)}, u32[]{:S(2)}, u32[]{:S(2)}) %collective-permute-start.1) | collective-permute-done | bytes 524320 | tf_op jit(solution)/shard_map/while/body/eval_jaxpr/ppermute | solution.py:15
  454.9 3.8 collective-permute-start.5
  458.7 7.7 %collective-permute-done.2 = bf16[512,512]{1,0:T(8,128)(2,1)S(1)} collective-permute-done((bf16[512,512]{1,0:T(8,128)(2,1)S(1)}, bf16[512,512]{1,0:T(8,128)(2,1)S(1)}, u32[]{:S(2)}, u32[]{:S(2)}) %collective-permute-start.2) | collective-permute-done | bytes 524320 | tf_op jit(solution)/shard_map/while/body/eval_jaxpr/ppermute | solution.py:15
  467.5 3.8 collective-permute-start.6
  471.2 8.2 %collective-permute-done.3 = bf16[512,512]{1,0:T(8,128)(2,1)} collective-permute-done((bf16[512,512]{1,0:T(8,128)(2,1)S(1)}, bf16[512,512]{1,0:T(8,128)(2,1)}, u32[]{:S(2)}, u32[]{:S(2)}) %collective-permute-start.3) | collective-permute-done | bytes 524320 | tf_op jit(solution)/shard_map/while/body/eval_jaxpr/ppermute | solution.py:15
  483.5 21.6 %fusion.19 = f32[512,4096]{1,0:T(8,128)S(1)} fusion(bf16[4096,4096]{1,0:T(8,128)(2,1)} %get-tuple-element.408, bf16[512,8192]{1,0:T(8,128)(2,1)S(1)} %constant_dynamic-update-slice_fusion.47, s32[]{:T(128)S(6)} %select_n.135), kind=kOutput, calls=%fused_computation.4.clone.1 | convolution fusion | flops 17179869184 | bytes 46137348 | tf_op jit(solution)/shard_map/while/body/eval_jaxpr/dot_general | solution.py:52
  505.1 8.1 %copy.12 = f32[64,8,8,512]{3,2,1,0:T(8,128)S(1)} copy(f32[64,8,8,512]{3,1,2,0:T(8,128)S(1)} %bitcast.31) | data formatting | bytes 16777216 | tf_op jit(solution)/shard_map/while
  513.3 3.9 fusion.21
  517.6 1.9 collective-permute-start.7
  519.5 10.0 %collective-permute-done.7 = bf16[512,512]{1,0:T(8,128)(2,1)S(1)} collective-permute-done((bf16[512,512]{1,0:T(8,128)(2,1)S(1)}, bf16[512,512]{1,0:T(8,128)(2,1)S(1)}, u32[]{:S(2)}, u32[]{:S(2)}) %collective-permute-start.7) | collective-permute-done | bytes 524320 | tf_op jit(solution)/shard_map/while/body/eval_jaxpr/ppermute | solution.py:25
  (179 shorter events, 37.6 us)
Async XLA Ops:
  0.6 23.8 %copy-start.2 = (f32[1,8,8]{2,1,0:T(8,128)S(1)}, f32[1,8,8]{2,1,0:T(8,128)}, u32[]{:S(2)}) copy-start(f32[1,8,8]{2,1,0:T(8,128)} %param.10) | copy-start | bytes 772
  0.6 23.8 %copy-start.3 = (f32[1,8,4]{1,2,0:T(4,128)S(1)}, f32[1,8,4]{1,2,0:T(4,128)}, u32[]{:S(2)}) copy-start(f32[1,8,4]{1,2,0:T(4,128)} %param.9) | copy-start | bytes 388
  0.7 23.8 %copy-start.5 = (s32[1,1024]{1,0:T(1,128)S(1)}, s32[1,1024]{1,0:T(1,128)}, u32[]{:S(2)}) copy-start(s32[1,1024]{1,0:T(1,128)} %param.11) | copy-start | bytes 12292
  25.7 10.5 %collective-permute-start = (bf16[512,512]{1,0:T(8,128)(2,1)S(1)}, bf16[512,512]{1,0:T(8,128)(2,1)S(1)}, u32[]{:S(2)}, u32[]{:S(2)}) collective-permute-start(bf16[512,512]{1,0:T(8,128)(2,1)S(1)} %dynamic-slice_select_fusion.2), channel_id=1, source_target_pairs={{0,1},{1,2},{2,3},{3,4},{4,5},{5,6},{6,7},{7,0},{8,9},{9,10},{10,1... | collective-permute-start | bytes 1572872 | tf_op jit(solution)/shard_map/while/body/eval_jaxpr/ppermute | solution.py:15
  36.2 15.7 %collective-permute-start.1 = (bf16[512,512]{1,0:T(8,128)(2,1)S(1)}, bf16[512,512]{1,0:T(8,128)(2,1)S(1)}, u32[]{:S(2)}, u32[]{:S(2)}) collective-permute-start(bf16[512,512]{1,0:T(8,128)(2,1)S(1)} %collective-permute-done), channel_id=1, source_target_pairs={{0,1},{1,2},{2,3},{3,4},{4,5},{5,6},{6,7},{7,0},{8,9},{9,10},{10,1... | collective-permute-start | bytes 1572872 | tf_op jit(solution)/shard_map/while/body/eval_jaxpr/ppermute | solution.py:15
  36.2 15.7 %collective-permute-start.4 = (bf16[512,512]{1,0:T(8,128)(2,1)S(1)}, bf16[512,512]{1,0:T(8,128)(2,1)S(1)}, u32[]{:S(2)}, u32[]{:S(2)}) collective-permute-start(bf16[512,512]{1,0:T(8,128)(2,1)S(1)} %dynamic-slice_select_fusion.2), channel_id=1, source_target_pairs={{0,7},{1,0},{2,1},{3,2},{4,3},{5,4},{6,5},{7,6},{8,15},{9,8},{10,9... | collective-permute-start | bytes 1572872 | tf_op jit(solution)/shard_map/while/body/eval_jaxpr/ppermute | solution.py:17
  51.9 14.6 %collective-permute-start.2 = (bf16[512,512]{1,0:T(8,128)(2,1)S(1)}, bf16[512,512]{1,0:T(8,128)(2,1)S(1)}, u32[]{:S(2)}, u32[]{:S(2)}) collective-permute-start(bf16[512,512]{1,0:T(8,128)(2,1)S(1)} %collective-permute-done.1), channel_id=1, source_target_pairs={{0,1},{1,2},{2,3},{3,4},{4,5},{5,6},{6,7},{7,0},{8,9},{9,10},{10,1... | collective-permute-start | bytes 1572872 | tf_op jit(solution)/shard_map/while/body/eval_jaxpr/ppermute | solution.py:15
  51.9 15.7 %collective-permute-start.5 = (bf16[512,512]{1,0:T(8,128)(2,1)S(1)}, bf16[512,512]{1,0:T(8,128)(2,1)S(1)}, u32[]{:S(2)}, u32[]{:S(2)}) collective-permute-start(bf16[512,512]{1,0:T(8,128)(2,1)S(1)} %collective-permute-done.4), channel_id=1, source_target_pairs={{0,7},{1,0},{2,1},{3,2},{4,3},{5,4},{6,5},{7,6},{8,15},{9,8},{10,9... | collective-permute-start | bytes 1572872 | tf_op jit(solution)/shard_map/while/body/eval_jaxpr/ppermute | solution.py:17
  66.5 13.1 %collective-permute-start.3 = (bf16[512,512]{1,0:T(8,128)(2,1)S(1)}, bf16[512,512]{1,0:T(8,128)(2,1)}, u32[]{:S(2)}, u32[]{:S(2)}) collective-permute-start(bf16[512,512]{1,0:T(8,128)(2,1)S(1)} %collective-permute-done.2), channel_id=1, source_target_pairs={{0,1},{1,2},{2,3},{3,4},{4,5},{5,6},{6,7},{7,0},{8,9},{9,10},{10,1... | collective-permute-start | bytes 1572872 | tf_op jit(solution)/shard_map/while/body/eval_jaxpr/ppermute | solution.py:15
  67.6 13.6 %collective-permute-start.6 = (bf16[512,512]{1,0:T(8,128)(2,1)S(1)}, bf16[512,512]{1,0:T(8,128)(2,1)S(1)}, u32[]{:S(2)}, u32[]{:S(2)}) collective-permute-start(bf16[512,512]{1,0:T(8,128)(2,1)S(1)} %collective-permute-done.5), channel_id=1, source_target_pairs={{0,7},{1,0},{2,1},{3,2},{4,3},{5,4},{6,5},{7,6},{8,15},{9,8},{10,9... | collective-permute-start | bytes 1572872 | tf_op jit(solution)/shard_map/while/body/eval_jaxpr/ppermute | solution.py:17
  113.4 4.1 copy-start
  117.8 12.0 %copy-start.1 = (bf16[1024,512]{1,0:T(8,128)(2,1)}, bf16[1024,512]{1,0:T(8,128)(2,1)S(1)}, u32[]{:S(2)}) copy-start(bf16[1024,512]{1,0:T(8,128)(2,1)S(1)} %get-tuple-element.401) | copy-start | bytes 3145732 | tf_op jit(solution)/shard_map/while
  117.8 12.0 %collective-permute-start.7 = (bf16[512,512]{1,0:T(8,128)(2,1)S(1)}, bf16[512,512]{1,0:T(8,128)(2,1)S(1)}, u32[]{:S(2)}, u32[]{:S(2)}) collective-permute-start(bf16[512,512]{1,0:T(8,128)(2,1)S(1)} %get-tuple-element.354), channel_id=1, source_target_pairs={{0,8},{8,16},{16,24},{1,9},{9,17},{17,25},{2,10},{10,18},{18,26},{... | collective-permute-start | bytes 1572872 | tf_op jit(solution)/shard_map/while/body/eval_jaxpr/ppermute | solution.py:25
  131.0 10.6 %collective-permute-start = (bf16[512,512]{1,0:T(8,128)(2,1)S(1)}, bf16[512,512]{1,0:T(8,128)(2,1)S(1)}, u32[]{:S(2)}, u32[]{:S(2)}) collective-permute-start(bf16[512,512]{1,0:T(8,128)(2,1)S(1)} %dynamic-slice_select_fusion.2), channel_id=1, source_target_pairs={{0,1},{1,2},{2,3},{3,4},{4,5},{5,6},{6,7},{7,0},{8,9},{9,10},{10,1... | collective-permute-start | bytes 1572872 | tf_op jit(solution)/shard_map/while/body/eval_jaxpr/ppermute | solution.py:15
  141.5 12.5 %collective-permute-start.1 = (bf16[512,512]{1,0:T(8,128)(2,1)S(1)}, bf16[512,512]{1,0:T(8,128)(2,1)S(1)}, u32[]{:S(2)}, u32[]{:S(2)}) collective-permute-start(bf16[512,512]{1,0:T(8,128)(2,1)S(1)} %collective-permute-done), channel_id=1, source_target_pairs={{0,1},{1,2},{2,3},{3,4},{4,5},{5,6},{6,7},{7,0},{8,9},{9,10},{10,1... | collective-permute-start | bytes 1572872 | tf_op jit(solution)/shard_map/while/body/eval_jaxpr/ppermute | solution.py:15
  141.5 13.5 %collective-permute-start.4 = (bf16[512,512]{1,0:T(8,128)(2,1)S(1)}, bf16[512,512]{1,0:T(8,128)(2,1)S(1)}, u32[]{:S(2)}, u32[]{:S(2)}) collective-permute-start(bf16[512,512]{1,0:T(8,128)(2,1)S(1)} %dynamic-slice_select_fusion.2), channel_id=1, source_target_pairs={{0,7},{1,0},{2,1},{3,2},{4,3},{5,4},{6,5},{7,6},{8,15},{9,8},{10,9... | collective-permute-start | bytes 1572872 | tf_op jit(solution)/shard_map/while/body/eval_jaxpr/ppermute | solution.py:17
  154.0 12.5 %collective-permute-start.2 = (bf16[512,512]{1,0:T(8,128)(2,1)S(1)}, bf16[512,512]{1,0:T(8,128)(2,1)S(1)}, u32[]{:S(2)}, u32[]{:S(2)}) collective-permute-start(bf16[512,512]{1,0:T(8,128)(2,1)S(1)} %collective-permute-done.1), channel_id=1, source_target_pairs={{0,1},{1,2},{2,3},{3,4},{4,5},{5,6},{6,7},{7,0},{8,9},{9,10},{10,1... | collective-permute-start | bytes 1572872 | tf_op jit(solution)/shard_map/while/body/eval_jaxpr/ppermute | solution.py:15
  155.1 12.5 %collective-permute-start.5 = (bf16[512,512]{1,0:T(8,128)(2,1)S(1)}, bf16[512,512]{1,0:T(8,128)(2,1)S(1)}, u32[]{:S(2)}, u32[]{:S(2)}) collective-permute-start(bf16[512,512]{1,0:T(8,128)(2,1)S(1)} %collective-permute-done.4), channel_id=1, source_target_pairs={{0,7},{1,0},{2,1},{3,2},{4,3},{5,4},{6,5},{7,6},{8,15},{9,8},{10,9... | collective-permute-start | bytes 1572872 | tf_op jit(solution)/shard_map/while/body/eval_jaxpr/ppermute | solution.py:17
  166.5 13.0 %collective-permute-start.3 = (bf16[512,512]{1,0:T(8,128)(2,1)S(1)}, bf16[512,512]{1,0:T(8,128)(2,1)}, u32[]{:S(2)}, u32[]{:S(2)}) collective-permute-start(bf16[512,512]{1,0:T(8,128)(2,1)S(1)} %collective-permute-done.2), channel_id=1, source_target_pairs={{0,1},{1,2},{2,3},{3,4},{4,5},{5,6},{6,7},{7,0},{8,9},{9,10},{10,1... | collective-permute-start | bytes 1572872 | tf_op jit(solution)/shard_map/while/body/eval_jaxpr/ppermute | solution.py:15
  167.6 13.5 %collective-permute-start.6 = (bf16[512,512]{1,0:T(8,128)(2,1)S(1)}, bf16[512,512]{1,0:T(8,128)(2,1)S(1)}, u32[]{:S(2)}, u32[]{:S(2)}) collective-permute-start(bf16[512,512]{1,0:T(8,128)(2,1)S(1)} %collective-permute-done.5), channel_id=1, source_target_pairs={{0,7},{1,0},{2,1},{3,2},{4,3},{5,4},{6,5},{7,6},{8,15},{9,8},{10,9... | collective-permute-start | bytes 1572872 | tf_op jit(solution)/shard_map/while/body/eval_jaxpr/ppermute | solution.py:17
  213.3 4.1 copy-start
  217.7 12.0 %copy-start.1 = (bf16[1024,512]{1,0:T(8,128)(2,1)}, bf16[1024,512]{1,0:T(8,128)(2,1)S(1)}, u32[]{:S(2)}) copy-start(bf16[1024,512]{1,0:T(8,128)(2,1)S(1)} %get-tuple-element.401) | copy-start | bytes 3145732 | tf_op jit(solution)/shard_map/while
  217.7 12.0 %collective-permute-start.7 = (bf16[512,512]{1,0:T(8,128)(2,1)S(1)}, bf16[512,512]{1,0:T(8,128)(2,1)S(1)}, u32[]{:S(2)}, u32[]{:S(2)}) collective-permute-start(bf16[512,512]{1,0:T(8,128)(2,1)S(1)} %get-tuple-element.354), channel_id=1, source_target_pairs={{0,8},{8,16},{16,24},{1,9},{9,17},{17,25},{2,10},{10,18},{18,26},{... | collective-permute-start | bytes 1572872 | tf_op jit(solution)/shard_map/while/body/eval_jaxpr/ppermute | solution.py:25
  230.9 10.6 %collective-permute-start = (bf16[512,512]{1,0:T(8,128)(2,1)S(1)}, bf16[512,512]{1,0:T(8,128)(2,1)S(1)}, u32[]{:S(2)}, u32[]{:S(2)}) collective-permute-start(bf16[512,512]{1,0:T(8,128)(2,1)S(1)} %dynamic-slice_select_fusion.2), channel_id=1, source_target_pairs={{0,1},{1,2},{2,3},{3,4},{4,5},{5,6},{6,7},{7,0},{8,9},{9,10},{10,1... | collective-permute-start | bytes 1572872 | tf_op jit(solution)/shard_map/while/body/eval_jaxpr/ppermute | solution.py:15
  241.5 12.4 %collective-permute-start.1 = (bf16[512,512]{1,0:T(8,128)(2,1)S(1)}, bf16[512,512]{1,0:T(8,128)(2,1)S(1)}, u32[]{:S(2)}, u32[]{:S(2)}) collective-permute-start(bf16[512,512]{1,0:T(8,128)(2,1)S(1)} %collective-permute-done), channel_id=1, source_target_pairs={{0,1},{1,2},{2,3},{3,4},{4,5},{5,6},{6,7},{7,0},{8,9},{9,10},{10,1... | collective-permute-start | bytes 1572872 | tf_op jit(solution)/shard_map/while/body/eval_jaxpr/ppermute | solution.py:15
  241.5 15.1 %collective-permute-start.4 = (bf16[512,512]{1,0:T(8,128)(2,1)S(1)}, bf16[512,512]{1,0:T(8,128)(2,1)S(1)}, u32[]{:S(2)}, u32[]{:S(2)}) collective-permute-start(bf16[512,512]{1,0:T(8,128)(2,1)S(1)} %dynamic-slice_select_fusion.2), channel_id=1, source_target_pairs={{0,7},{1,0},{2,1},{3,2},{4,3},{5,4},{6,5},{7,6},{8,15},{9,8},{10,9... | collective-permute-start | bytes 1572872 | tf_op jit(solution)/shard_map/while/body/eval_jaxpr/ppermute | solution.py:17
  253.9 12.5 %collective-permute-start.2 = (bf16[512,512]{1,0:T(8,128)(2,1)S(1)}, bf16[512,512]{1,0:T(8,128)(2,1)S(1)}, u32[]{:S(2)}, u32[]{:S(2)}) collective-permute-start(bf16[512,512]{1,0:T(8,128)(2,1)S(1)} %collective-permute-done.1), channel_id=1, source_target_pairs={{0,1},{1,2},{2,3},{3,4},{4,5},{5,6},{6,7},{7,0},{8,9},{9,10},{10,1... | collective-permute-start | bytes 1572872 | tf_op jit(solution)/shard_map/while/body/eval_jaxpr/ppermute | solution.py:15
  256.6 13.5 %collective-permute-start.5 = (bf16[512,512]{1,0:T(8,128)(2,1)S(1)}, bf16[512,512]{1,0:T(8,128)(2,1)S(1)}, u32[]{:S(2)}, u32[]{:S(2)}) collective-permute-start(bf16[512,512]{1,0:T(8,128)(2,1)S(1)} %collective-permute-done.4), channel_id=1, source_target_pairs={{0,7},{1,0},{2,1},{3,2},{4,3},{5,4},{6,5},{7,6},{8,15},{9,8},{10,9... | collective-permute-start | bytes 1572872 | tf_op jit(solution)/shard_map/while/body/eval_jaxpr/ppermute | solution.py:17
  266.4 13.0 %collective-permute-start.3 = (bf16[512,512]{1,0:T(8,128)(2,1)S(1)}, bf16[512,512]{1,0:T(8,128)(2,1)}, u32[]{:S(2)}, u32[]{:S(2)}) collective-permute-start(bf16[512,512]{1,0:T(8,128)(2,1)S(1)} %collective-permute-done.2), channel_id=1, source_target_pairs={{0,1},{1,2},{2,3},{3,4},{4,5},{5,6},{6,7},{7,0},{8,9},{9,10},{10,1... | collective-permute-start | bytes 1572872 | tf_op jit(solution)/shard_map/while/body/eval_jaxpr/ppermute | solution.py:15
  270.0 10.9 %collective-permute-start.6 = (bf16[512,512]{1,0:T(8,128)(2,1)S(1)}, bf16[512,512]{1,0:T(8,128)(2,1)S(1)}, u32[]{:S(2)}, u32[]{:S(2)}) collective-permute-start(bf16[512,512]{1,0:T(8,128)(2,1)S(1)} %collective-permute-done.5), channel_id=1, source_target_pairs={{0,7},{1,0},{2,1},{3,2},{4,3},{5,4},{6,5},{7,6},{8,15},{9,8},{10,9... | collective-permute-start | bytes 1572872 | tf_op jit(solution)/shard_map/while/body/eval_jaxpr/ppermute | solution.py:17
  313.2 4.1 copy-start
  317.6 12.0 %copy-start.1 = (bf16[1024,512]{1,0:T(8,128)(2,1)}, bf16[1024,512]{1,0:T(8,128)(2,1)S(1)}, u32[]{:S(2)}) copy-start(bf16[1024,512]{1,0:T(8,128)(2,1)S(1)} %get-tuple-element.401) | copy-start | bytes 3145732 | tf_op jit(solution)/shard_map/while
  317.6 12.0 %collective-permute-start.7 = (bf16[512,512]{1,0:T(8,128)(2,1)S(1)}, bf16[512,512]{1,0:T(8,128)(2,1)S(1)}, u32[]{:S(2)}, u32[]{:S(2)}) collective-permute-start(bf16[512,512]{1,0:T(8,128)(2,1)S(1)} %get-tuple-element.354), channel_id=1, source_target_pairs={{0,8},{8,16},{16,24},{1,9},{9,17},{17,25},{2,10},{10,18},{18,26},{... | collective-permute-start | bytes 1572872 | tf_op jit(solution)/shard_map/while/body/eval_jaxpr/ppermute | solution.py:25
  330.8 10.6 %collective-permute-start = (bf16[512,512]{1,0:T(8,128)(2,1)S(1)}, bf16[512,512]{1,0:T(8,128)(2,1)S(1)}, u32[]{:S(2)}, u32[]{:S(2)}) collective-permute-start(bf16[512,512]{1,0:T(8,128)(2,1)S(1)} %dynamic-slice_select_fusion.2), channel_id=1, source_target_pairs={{0,1},{1,2},{2,3},{3,4},{4,5},{5,6},{6,7},{7,0},{8,9},{9,10},{10,1... | collective-permute-start | bytes 1572872 | tf_op jit(solution)/shard_map/while/body/eval_jaxpr/ppermute | solution.py:15
  341.3 12.5 %collective-permute-start.1 = (bf16[512,512]{1,0:T(8,128)(2,1)S(1)}, bf16[512,512]{1,0:T(8,128)(2,1)S(1)}, u32[]{:S(2)}, u32[]{:S(2)}) collective-permute-start(bf16[512,512]{1,0:T(8,128)(2,1)S(1)} %collective-permute-done), channel_id=1, source_target_pairs={{0,1},{1,2},{2,3},{3,4},{4,5},{5,6},{6,7},{7,0},{8,9},{9,10},{10,1... | collective-permute-start | bytes 1572872 | tf_op jit(solution)/shard_map/while/body/eval_jaxpr/ppermute | solution.py:15
  341.3 13.6 %collective-permute-start.4 = (bf16[512,512]{1,0:T(8,128)(2,1)S(1)}, bf16[512,512]{1,0:T(8,128)(2,1)S(1)}, u32[]{:S(2)}, u32[]{:S(2)}) collective-permute-start(bf16[512,512]{1,0:T(8,128)(2,1)S(1)} %dynamic-slice_select_fusion.2), channel_id=1, source_target_pairs={{0,7},{1,0},{2,1},{3,2},{4,3},{5,4},{6,5},{7,6},{8,15},{9,8},{10,9... | collective-permute-start | bytes 1572872 | tf_op jit(solution)/shard_map/while/body/eval_jaxpr/ppermute | solution.py:17
  353.9 12.5 %collective-permute-start.2 = (bf16[512,512]{1,0:T(8,128)(2,1)S(1)}, bf16[512,512]{1,0:T(8,128)(2,1)S(1)}, u32[]{:S(2)}, u32[]{:S(2)}) collective-permute-start(bf16[512,512]{1,0:T(8,128)(2,1)S(1)} %collective-permute-done.1), channel_id=1, source_target_pairs={{0,1},{1,2},{2,3},{3,4},{4,5},{5,6},{6,7},{7,0},{8,9},{9,10},{10,1... | collective-permute-start | bytes 1572872 | tf_op jit(solution)/shard_map/while/body/eval_jaxpr/ppermute | solution.py:15
  354.9 12.5 %collective-permute-start.5 = (bf16[512,512]{1,0:T(8,128)(2,1)S(1)}, bf16[512,512]{1,0:T(8,128)(2,1)S(1)}, u32[]{:S(2)}, u32[]{:S(2)}) collective-permute-start(bf16[512,512]{1,0:T(8,128)(2,1)S(1)} %collective-permute-done.4), channel_id=1, source_target_pairs={{0,7},{1,0},{2,1},{3,2},{4,3},{5,4},{6,5},{7,6},{8,15},{9,8},{10,9... | collective-permute-start | bytes 1572872 | tf_op jit(solution)/shard_map/while/body/eval_jaxpr/ppermute | solution.py:17
  366.4 13.1 %collective-permute-start.3 = (bf16[512,512]{1,0:T(8,128)(2,1)S(1)}, bf16[512,512]{1,0:T(8,128)(2,1)}, u32[]{:S(2)}, u32[]{:S(2)}) collective-permute-start(bf16[512,512]{1,0:T(8,128)(2,1)S(1)} %collective-permute-done.2), channel_id=1, source_target_pairs={{0,1},{1,2},{2,3},{3,4},{4,5},{5,6},{6,7},{7,0},{8,9},{9,10},{10,1... | collective-permute-start | bytes 1572872 | tf_op jit(solution)/shard_map/while/body/eval_jaxpr/ppermute | solution.py:15
  367.4 13.5 %collective-permute-start.6 = (bf16[512,512]{1,0:T(8,128)(2,1)S(1)}, bf16[512,512]{1,0:T(8,128)(2,1)S(1)}, u32[]{:S(2)}, u32[]{:S(2)}) collective-permute-start(bf16[512,512]{1,0:T(8,128)(2,1)S(1)} %collective-permute-done.5), channel_id=1, source_target_pairs={{0,7},{1,0},{2,1},{3,2},{4,3},{5,4},{6,5},{7,6},{8,15},{9,8},{10,9... | collective-permute-start | bytes 1572872 | tf_op jit(solution)/shard_map/while/body/eval_jaxpr/ppermute | solution.py:17
  413.2 4.1 copy-start
  417.6 12.0 %copy-start.1 = (bf16[1024,512]{1,0:T(8,128)(2,1)}, bf16[1024,512]{1,0:T(8,128)(2,1)S(1)}, u32[]{:S(2)}) copy-start(bf16[1024,512]{1,0:T(8,128)(2,1)S(1)} %get-tuple-element.401) | copy-start | bytes 3145732 | tf_op jit(solution)/shard_map/while
  417.6 12.0 %collective-permute-start.7 = (bf16[512,512]{1,0:T(8,128)(2,1)S(1)}, bf16[512,512]{1,0:T(8,128)(2,1)S(1)}, u32[]{:S(2)}, u32[]{:S(2)}) collective-permute-start(bf16[512,512]{1,0:T(8,128)(2,1)S(1)} %get-tuple-element.354), channel_id=1, source_target_pairs={{0,8},{8,16},{16,24},{1,9},{9,17},{17,25},{2,10},{10,18},{18,26},{... | collective-permute-start | bytes 1572872 | tf_op jit(solution)/shard_map/while/body/eval_jaxpr/ppermute | solution.py:25
  430.8 10.5 %collective-permute-start = (bf16[512,512]{1,0:T(8,128)(2,1)S(1)}, bf16[512,512]{1,0:T(8,128)(2,1)S(1)}, u32[]{:S(2)}, u32[]{:S(2)}) collective-permute-start(bf16[512,512]{1,0:T(8,128)(2,1)S(1)} %dynamic-slice_select_fusion.2), channel_id=1, source_target_pairs={{0,1},{1,2},{2,3},{3,4},{4,5},{5,6},{6,7},{7,0},{8,9},{9,10},{10,1... | collective-permute-start | bytes 1572872 | tf_op jit(solution)/shard_map/while/body/eval_jaxpr/ppermute | solution.py:15
  441.3 12.6 %collective-permute-start.1 = (bf16[512,512]{1,0:T(8,128)(2,1)S(1)}, bf16[512,512]{1,0:T(8,128)(2,1)S(1)}, u32[]{:S(2)}, u32[]{:S(2)}) collective-permute-start(bf16[512,512]{1,0:T(8,128)(2,1)S(1)} %collective-permute-done), channel_id=1, source_target_pairs={{0,1},{1,2},{2,3},{3,4},{4,5},{5,6},{6,7},{7,0},{8,9},{9,10},{10,1... | collective-permute-start | bytes 1572872 | tf_op jit(solution)/shard_map/while/body/eval_jaxpr/ppermute | solution.py:15
  441.3 13.6 %collective-permute-start.4 = (bf16[512,512]{1,0:T(8,128)(2,1)S(1)}, bf16[512,512]{1,0:T(8,128)(2,1)S(1)}, u32[]{:S(2)}, u32[]{:S(2)}) collective-permute-start(bf16[512,512]{1,0:T(8,128)(2,1)S(1)} %dynamic-slice_select_fusion.2), channel_id=1, source_target_pairs={{0,7},{1,0},{2,1},{3,2},{4,3},{5,4},{6,5},{7,6},{8,15},{9,8},{10,9... | collective-permute-start | bytes 1572872 | tf_op jit(solution)/shard_map/while/body/eval_jaxpr/ppermute | solution.py:17
  453.9 12.5 %collective-permute-start.2 = (bf16[512,512]{1,0:T(8,128)(2,1)S(1)}, bf16[512,512]{1,0:T(8,128)(2,1)S(1)}, u32[]{:S(2)}, u32[]{:S(2)}) collective-permute-start(bf16[512,512]{1,0:T(8,128)(2,1)S(1)} %collective-permute-done.1), channel_id=1, source_target_pairs={{0,1},{1,2},{2,3},{3,4},{4,5},{5,6},{6,7},{7,0},{8,9},{9,10},{10,1... | collective-permute-start | bytes 1572872 | tf_op jit(solution)/shard_map/while/body/eval_jaxpr/ppermute | solution.py:15
  454.9 12.6 %collective-permute-start.5 = (bf16[512,512]{1,0:T(8,128)(2,1)S(1)}, bf16[512,512]{1,0:T(8,128)(2,1)S(1)}, u32[]{:S(2)}, u32[]{:S(2)}) collective-permute-start(bf16[512,512]{1,0:T(8,128)(2,1)S(1)} %collective-permute-done.4), channel_id=1, source_target_pairs={{0,7},{1,0},{2,1},{3,2},{4,3},{5,4},{6,5},{7,6},{8,15},{9,8},{10,9... | collective-permute-start | bytes 1572872 | tf_op jit(solution)/shard_map/while/body/eval_jaxpr/ppermute | solution.py:17
  466.4 13.1 %collective-permute-start.3 = (bf16[512,512]{1,0:T(8,128)(2,1)S(1)}, bf16[512,512]{1,0:T(8,128)(2,1)}, u32[]{:S(2)}, u32[]{:S(2)}) collective-permute-start(bf16[512,512]{1,0:T(8,128)(2,1)S(1)} %collective-permute-done.2), channel_id=1, source_target_pairs={{0,1},{1,2},{2,3},{3,4},{4,5},{5,6},{6,7},{7,0},{8,9},{9,10},{10,1... | collective-permute-start | bytes 1572872 | tf_op jit(solution)/shard_map/while/body/eval_jaxpr/ppermute | solution.py:15
  467.5 13.5 %collective-permute-start.6 = (bf16[512,512]{1,0:T(8,128)(2,1)S(1)}, bf16[512,512]{1,0:T(8,128)(2,1)S(1)}, u32[]{:S(2)}, u32[]{:S(2)}) collective-permute-start(bf16[512,512]{1,0:T(8,128)(2,1)S(1)} %collective-permute-done.5), channel_id=1, source_target_pairs={{0,7},{1,0},{2,1},{3,2},{4,3},{5,4},{6,5},{7,6},{8,15},{9,8},{10,9... | collective-permute-start | bytes 1572872 | tf_op jit(solution)/shard_map/while/body/eval_jaxpr/ppermute | solution.py:17
  513.2 4.1 copy-start
  517.6 12.0 %copy-start.1 = (bf16[1024,512]{1,0:T(8,128)(2,1)}, bf16[1024,512]{1,0:T(8,128)(2,1)S(1)}, u32[]{:S(2)}) copy-start(bf16[1024,512]{1,0:T(8,128)(2,1)S(1)} %get-tuple-element.401) | copy-start | bytes 3145732 | tf_op jit(solution)/shard_map/while
  517.6 12.0 %collective-permute-start.7 = (bf16[512,512]{1,0:T(8,128)(2,1)S(1)}, bf16[512,512]{1,0:T(8,128)(2,1)S(1)}, u32[]{:S(2)}, u32[]{:S(2)}) collective-permute-start(bf16[512,512]{1,0:T(8,128)(2,1)S(1)} %get-tuple-element.354), channel_id=1, source_target_pairs={{0,8},{8,16},{16,24},{1,9},{9,17},{17,25},{2,10},{10,18},{18,26},{... | collective-permute-start | bytes 1572872 | tf_op jit(solution)/shard_map/while/body/eval_jaxpr/ppermute | solution.py:25
  529.6 0.6 copy-start.4
